TPU v7x, 32 devices: a whole 2x2x4 slice. The times are simulated.
32 devices in a mesh: groups: 2 (over y), seq: 8 (over z, core), section: 2 (over x), tp: 1.
Axes of the slice: x: 2, y: 2, z: 4, core: 2. Of those that a mesh axis runs over, the one named last changes fastest.
Arguments:
- stream: bfloat16 [4, 512, 1536], P('groups', 'seq', 'tp'), parts along dimension 0, may hold values from -30 to 30
- set_views: int32 [4, 6], P('groups'), parts along dimension 0, may hold values from 1 to 2, 8 in all within a row
- modulation: bfloat16 [2, 4, 6, 2, 1536], P('section', 'groups', None, None, 'tp'), parts along dimension 1, may hold values from -2.5 to 2.5
- set_gate: bfloat16 [2, 4, 6, 1536], P('section', 'groups', None, 'tp'), parts along dimension 1, may hold values from 0.5 to 1.5
- qkv_weight: bfloat16 [2, 1536, 3, 1536], P('section', 'seq', None, 'tp'), may hold values from -0.15625 to 0.15625
- norm_gain: float32 [2, 2, 128], P('section'), may hold values from 0.1 to 1.9
- out_weight: bfloat16 [2, 1536, 1536], P('section', None, 'tp'), may hold values from -0.15625 to 0.15625
Outputs:
- hidden: bfloat16 [2, 4, 512, 1536], P('section', 'groups', 'seq', 'tp'), parts along dimension 1
There are 2 independent parts, one for each index of `groups`. A program takes and returns all parts, laid end to end along the dimension named above; an argument that names none is the same for every part. Nothing has to cross between parts.
Inputs may be any that keep to these rules, and one draw needn't show every extreme that they name: Each row of set_views sums to 8; every row has a set of 2 views.
All inputs are finite; a program needn't handle non-finite values.
Results may differ from a plain program's by a relative error of at most 0.01.
Values may be sent and summed in bfloat16 or wider, within the bound.
No kernel may reach another device: no remote copies, remote signals or barrier semaphores. Data moves between devices by JAX's collectives and lax.ppermute only.
A program may use at most 64 MiB of HBM per device.

v0:
```python
import jax
import jax.numpy as jnp
from jax import lax
from jax.sharding import PartitionSpec as P

REACH = 1
epsilon = 1e-06


def shifted(array, axis, by):
    size = lax.axis_size(axis)
    pairs = [(i, i + by) for i in range(size) if 0 <= i + by < size]
    return lax.ppermute(array, axis, pairs)


def view_sets(set_views, count):
    starts = jnp.cumsum(set_views) - set_views
    position = jnp.arange(count, dtype=jnp.int32)
    inside = (starts[None, :] <= position[:, None]).astype(jnp.int32)
    return jnp.sum(inside, axis=1) - 1


def unit_rms(values, scaling):
    return values * lax.rsqrt(jnp.mean(values * values, axis=-1, keepdims=True) + epsilon) * scaling


def relay_cycle(payload):
    moving = payload
    moving = shifted(moving, "seq", 1)
    below_list = [moving]
    moving = payload
    moving = shifted(moving, "seq", -1)
    above_list = [moving]
    return below_list[::-1] + [payload] + above_list


def body(stream, set_views, modulation, set_gate, qkv_weight, norm_gain, out_weight):
    micro_count, view_tok, local_width = stream.shape
    head_size = norm_gain.shape[2]
    head_count = local_width // head_size
    seq_count = lax.axis_size("seq")
    section_count = lax.axis_size("section")
    seq_place = lax.axis_index("seq")
    section_place = lax.axis_index("section")
    full_width = local_width * lax.axis_size("tp")
    whole_qkv = lax.all_gather(qkv_weight[0], "seq", axis=0, tiled=True)
    qkv_flat = whole_qkv.reshape(whole_qkv.shape[0], 3 * local_width)
    gain_pair = norm_gain[0]
    out_rows = out_weight[0]
    score_scale = head_size ** (-0.5)
    offsets = list(range(-REACH, REACH + 1))
    ticks = micro_count + section_count - 1
    carried = jnp.zeros((view_tok, local_width), jnp.bfloat16)
    hidden = jnp.zeros((micro_count, view_tok, local_width), jnp.bfloat16)
    for moment in range(ticks):
        fresh_input = stream[min(moment, micro_count - 1)]
        section_input = jnp.where(section_place == 0, fresh_input, carried)
        micro_raw = moment - section_place
        micro_index = jnp.clip(micro_raw, 0, micro_count - 1)
        owners = view_sets(set_views[micro_index], seq_count)
        own_set = owners[seq_place]
        widened = section_input.astype(jnp.float32)
        totals, squares = lax.psum(
            (jnp.sum(widened, axis=1), jnp.sum(widened * widened, axis=1)), "tp"
        )
        average = (totals / full_width)[:, None]
        spread = (squares / full_width)[:, None] - average * average
        factors = modulation[0, micro_index, own_set].astype(jnp.float32)
        normed = (
            (widened - average) * lax.rsqrt(spread + epsilon) * (1.0 + factors[1]) + factors[0]
        ).astype(jnp.bfloat16)
        section_projected = jnp.dot(
            lax.all_gather(normed, "tp", axis=1, tiled=True),
            qkv_flat,
            preferred_element_type=jnp.float32,
        )
        queries = unit_rms(
            section_projected.reshape(view_tok, 3, head_count, head_size)[:, 0], gain_pair[0]
        ).astype(jnp.bfloat16)
        parts = section_projected.reshape(view_tok, 3, head_count, head_size)
        keys_here = unit_rms(parts[:, 1], gain_pair[1]).astype(jnp.bfloat16)
        values_here = parts[:, 2].astype(jnp.bfloat16)
        key_list = []
        value_list = []
        stacked = jnp.stack(
            [keys_here.reshape(view_tok, local_width), values_here.reshape(view_tok, local_width)]
        )
        arrived = relay_cycle(stacked)
        for received in arrived:
            key_list.append(received[0].reshape(view_tok, head_count, head_size))
            value_list.append(received[1].reshape(view_tok, head_count, head_size))
        visible = []
        for offset in offsets:
            neighbour = seq_place + offset
            in_range = (neighbour >= 0) & (neighbour < seq_count)
            same_set = owners[jnp.clip(neighbour, 0, seq_count - 1)] == own_set
            visible.append((in_range & same_set).astype(jnp.float32))
        keys_cat = jnp.concatenate(key_list, axis=0)
        values_cat = jnp.concatenate(value_list, axis=0)
        mask_row = jnp.repeat(jnp.stack(visible), view_tok)
        scores = (
            jnp.einsum("qhd,khd->hqk", queries, keys_cat, preferred_element_type=jnp.float32)
            * score_scale
        )
        exponent = jnp.exp(scores) * mask_row
        denominator = jnp.sum(exponent, axis=-1)
        numerator = jnp.einsum(
            "hqk,khd->qhd",
            exponent.astype(jnp.bfloat16),
            values_cat,
            preferred_element_type=jnp.float32,
        )
        attended = (
            (numerator / jnp.transpose(denominator)[:, :, None])
            .astype(jnp.bfloat16)
            .reshape(view_tok, local_width)
        )
        mixed_out = jnp.dot(
            lax.all_gather(attended, "tp", axis=1, tiled=True),
            out_rows,
            preferred_element_type=jnp.float32,
        )
        gating = set_gate[0, micro_index, own_set].astype(jnp.float32)
        result = (widened + gating * mixed_out).astype(jnp.bfloat16)
        in_range = (micro_raw >= 0) & (micro_raw < micro_count)
        hidden = jnp.where(in_range, hidden.at[micro_index].set(result), hidden)
        if moment + 1 < ticks:
            carried = shifted(result, "section", 1)
    return hidden[None]


def solution(mesh):
    placed = (
        P("groups", "seq", "tp"),
        P("groups", None),
        P("section", "groups", None, None, "tp"),
        P("section", "groups", None, "tp"),
        P("section", "seq", None, "tp"),
        P("section", None, None),
        P("section", None, "tp"),
    )
    return jax.shard_map(
        body,
        mesh=mesh,
        in_specs=placed,
        out_specs=P("section", "groups", "seq", "tp"),
        check_vma=False,
    )
```

profile of v0, /device:TPU:10, one launch (start us, length us, event | category | flops | bytes accessed | tf_op | source)
XLA Modules:
  0.0 268.0 jit_solution(7791036206823551094)
XLA Ops:
  25.9 111.1 %all-gather.3.cloned.1.call-done = bf16[1,1536,3,1536]{3,1,2,0:T(8,128)(2,1)} async-done(((bf16[1,192,3,1536]{3,1,2,0:T(8,128)(2,1)}), bf16[1,1536,3,1536]{3,1,2,0:T(8,128)(2,1)}) %all-gather.3.cloned.1.call-update) | async-done | bytes 14155792 | tf_op jit(solution)/shard_map/all_gather | solution.py:46
  137.0 18.7 %copy.58 = bf16[1,1536,3,1536]{1,3,2,0:T(8,128)(2,1)} copy(bf16[1,1536,3,1536]{3,1,2,0:T(8,128)(2,1)} %all-gather.3.cloned.1.call-done) | data formatting | bytes 28311552 | tf_op jit(solution)/shard_map/all_gather | solution.py:46
  155.7 7.6 %fusion.129 = f32[64,3,12,128]{3,0,2,1:T(8,128)S(1)} fusion(bf16[3,12,128,1536]{3,2,1,0:T(8,128)(2,1)} %bitcast.253, f32[1536]{0:T(1024)S(1)} %get-tuple-element.59, f32[1536]{0:T(1024)S(1)} %get-tuple-element.58, f32[64]{0:T(128)S(1)} %get-tuple-element.102, f32[64]{0:T(128)S(1)} %get-tuple-element.101, bf16[2,64,1536]{2,1,0:T(8,128)(2,1)S(1)} %copy-done.6, ...), kind=kOutput, calls=%fused_computation.139 | convolution fusion | flops 906657792 | bytes 15549441 | tf_op jit(solution)/shard_map/dot_general | solution.py:72
  166.1 5.2 %collective-permute-start.1 = (bf16[2,64,1536]{2,1,0:T(8,128)(2,1)S(1)}, bf16[2,64,1536]{2,1,0:T(8,128)(2,1)S(1)}, u32[]{:S(2)}, u32[]{:S(2)}) collective-permute-start(bf16[2,64,1536]{2,1,0:T(8,128)(2,1)S(1)} %pad_maximum_fusion), channel_id=1, source_target_pairs={{2,0},{4,2},{6,4},{8,6},{10,8},{12,10},{14,12},{3,1},{5,3},{7,5},{... | collective-permute-start | bytes 1179656 | tf_op jit(solution)/shard_map/ppermute | solution.py:13
  171.3 1.9 collective-permute-start
  173.2 0.8 fusion.117
  174.1 2.5 collective-permute-done.1
  177.0 3.4 %collective-permute-done = bf16[2,64,1536]{2,1,0:T(8,128)(2,1)S(1)} collective-permute-done((bf16[2,64,1536]{2,1,0:T(8,128)(2,1)S(1)}, bf16[2,64,1536]{2,1,0:T(8,128)(2,1)S(1)}, u32[]{:S(2)}, u32[]{:S(2)}) %collective-permute-start) | collective-permute-done | bytes 393248 | tf_op jit(solution)/shard_map/ppermute | solution.py:13
  182.6 3.9 %bitcast_dynamic-update-slice_fusion = (bf16[2,64,1536]{2,1,0:T(8,128)(2,1)S(1)}, bf16[64,1536]{1,0:T(8,128)(2,1)S(1)}) fusion(bf16[2,64,1536]{2,1,0:T(8,128)(2,1)S(1)} %broadcast_in_dim.16, s32[]{:T(128)} %min.31, pred[]{:T(512)} %get-tuple-element.90, pred[]{:T(512)S(6)} %and.71, bf16[1,1536,1536]{2,1,0:T(8,128)(2,1)} %param.19, ...), kind=kOutput, calls=%fused_computation.148 | convolution fusion | flops 302678016 | bytes 5513223 | tf_op jit(solution)/shard_map/dot_general | solution.py:118
  186.5 1.3 collective-permute-start.2
  191.6 2.5 collective-permute-done.2
  194.3 7.6 %fusion.126 = f32[64,3,12,128]{3,0,2,1:T(8,128)S(1)} fusion(bf16[3,12,128,1536]{3,2,1,0:T(8,128)(2,1)} %bitcast.254, bf16[64,1536]{1,0:T(8,128)(2,1)S(1)} %get-tuple-element.63, f32[1536]{0:T(1024)S(1)} %get-tuple-element.57, f32[1536]{0:T(1024)S(1)} %get-tuple-element.56, f32[64]{0:T(128)S(1)} %get-tuple-element.96, f32[64]{0:T(128)S(1)} %get-tuple-element.95), kind=kOutput, calls=%fused_computation.137 | convolution fusion | flops 906559488 | bytes 15544832 | tf_op jit(solution)/shard_map/dot_general | solution.py:72
  203.2 0.8 convert_element_type.230
  204.7 1.0 pad_maximum_fusion.1
  205.7 1.9 collective-permute-start.4
  207.7 2.4 collective-permute-start.3
  210.1 0.8 fusion.114
  211.0 2.0 collective-permute-done.4
  214.1 2.8 %collective-permute-done.3 = bf16[2,64,1536]{2,1,0:T(8,128)(2,1)} collective-permute-done((bf16[2,64,1536]{2,1,0:T(8,128)(2,1)S(1)}, bf16[2,64,1536]{2,1,0:T(8,128)(2,1)}, u32[]{:S(2)}, u32[]{:S(2)}) %collective-permute-start.3) | collective-permute-done | bytes 393248 | tf_op jit(solution)/shard_map/ppermute | solution.py:13
  216.9 1.0 fusion.167
  218.4 1.6 fusion.175
  220.3 4.0 %fusion.121 = (bf16[2,64,1536]{2,1,0:T(8,128)(2,1)S(1)}, bf16[64,1536]{1,0:T(8,128)(2,1)S(1)}) fusion(bf16[2,64,1536]{2,1,0:T(8,128)(2,1)S(1)} %get-tuple-element.107, s32[]{:T(128)} %min.36, pred[]{:T(512)} %get-tuple-element.61, pred[]{:T(512)S(6)} %and.79, bf16[1,1536,1536]{2,1,0:T(8,128)(2,1)} %param.19, bf16[12,8,8,128]{3,2,1,0:T(8,128)(2,1)S(1)} %fusion.61, ...), kind=kOutput, calls=%fused_computation.133 | convolution fusion | flops 302579712 | bytes 5709830 | tf_op jit(solution)/shard_map/dot_general | solution.py:118
  224.3 1.5 collective-permute-start.5
  226.8 5.1 %collective-permute-done.5 = bf16[64,1536]{1,0:T(8,128)(2,1)S(1)} collective-permute-done((bf16[64,1536]{1,0:T(8,128)(2,1)S(1)}, bf16[64,1536]{1,0:T(8,128)(2,1)S(1)}, u32[]{:S(2)}, u32[]{:S(2)}) %collective-permute-start.5) | collective-permute-done | bytes 196640 | tf_op jit(solution)/shard_map/ppermute | solution.py:13
  232.1 7.6 %fusion.123 = f32[64,3,12,128]{3,0,2,1:T(8,128)S(1)} fusion(bf16[3,12,128,1536]{3,2,1,0:T(8,128)(2,1)} %bitcast.255, bf16[64,1536]{1,0:T(8,128)(2,1)S(1)} %get-tuple-element.62, f32[1536]{0:T(1024)S(1)} %get-tuple-element.55, f32[1536]{0:T(1024)S(1)} %get-tuple-element.54, f32[64]{0:T(128)S(1)} %get-tuple-element.89, f32[64]{0:T(128)S(1)} %get-tuple-element.88), kind=kOutput, calls=%fused_computation.135 | convolution fusion | flops 906559488 | bytes 15544832 | tf_op jit(solution)/shard_map/dot_general | solution.py:72
  242.5 2.1 collective-permute-start.7
  244.5 2.4 collective-permute-start.6
  247.0 0.8 fusion.111
  247.8 2.0 collective-permute-done.7
  251.6 2.0 collective-permute-done.6
  254.6 1.6 fusion.176
  256.5 4.6 %fusion.45 = bf16[1,2,64,1536]{3,2,1,0:T(8,128)(2,1)} fusion(bf16[1,2,64,1536]{3,2,1,0:T(8,128)(2,1)} %copy.110, s32[]{:T(128)} %min.38, bf16[1,1536,1536]{2,1,0:T(8,128)(2,1)} %param.19, bf16[64,1536]{1,0:T(8,128)(2,1)S(1)} %get-tuple-element.62, bf16[12,8,8,128]{3,2,1,0:T(8,128)(2,1)S(1)} %fusion.62, bf16[2,64,1536]{2,1,0:T(8,128)(2,1)S(1)} %get-tuple-element.109, ...), kind=kOutput, calls=%fused_computation.19 | convolution fusion | flops 302579712 | bytes 5512193 | tf_op jit(solution)/shard_map/dot_general | solution.py:118
  (158 shorter events, 22.4 us)
Async XLA Ops:
  6.5 17.4 %copy-start.17 = (s32[3]{0:T(128)S(1)}, s32[3]{0:T(128)}, u32[]{:S(2)}) copy-start(s32[3]{0:T(128)} %constant.115.clone.1) | copy-start | bytes 40
  6.5 0.8 copy-start.15
  6.5 17.3 %copy-start.14 = (bf16[1,2,6,1536]{3,1,2,0:T(2,128)(2,1)S(1)}, bf16[1,2,6,1536]{3,1,2,0:T(2,128)(2,1)}, u32[]{:S(2)}) copy-start(bf16[1,2,6,1536]{3,1,2,0:T(2,128)(2,1)} %param.16) | copy-start | bytes 110596
  6.5 19.0 %copy-start.6 = (bf16[2,64,1536]{2,1,0:T(8,128)(2,1)S(1)}, bf16[2,64,1536]{2,1,0:T(8,128)(2,1)}, u32[]{:S(2)}) copy-start(bf16[2,64,1536]{2,1,0:T(8,128)(2,1)} %param.13) | copy-start | bytes 1179652
  6.5 19.4 %copy-start.16 = (f32[1,2,128]{2,1,0:T(2,128)S(1)}, f32[1,2,128]{2,1,0:T(2,128)}, u32[]{:S(2)}) copy-start(f32[1,2,128]{2,1,0:T(2,128)} %param.18) | copy-start | bytes 3076
  6.5 130.5 %all-gather.3.cloned.1.call-start = ((), (), s32[]{:S(2)}) async-start(), calls=%async_computation | async-start | bytes 15925248 | tf_op jit(solution)/shard_map/all_gather | solution.py:46
  163.3 1.1 copy-start.2
  164.4 1.0 slice-start.1
  165.9 7.3 %copy-start.3 = (f32[64,3,12,128]{3,0,2,1:T(8,128)S(1)}, f32[64,3,12,128]{3,0,2,1:T(8,128)}, u32[]{:S(2)}) copy-start(f32[64,3,12,128]{3,0,2,1:T(8,128)} %copy-done.2) | copy-start | bytes 3538948
  166.1 10.5 %collective-permute-start.1 = (bf16[2,64,1536]{2,1,0:T(8,128)(2,1)S(1)}, bf16[2,64,1536]{2,1,0:T(8,128)(2,1)S(1)}, u32[]{:S(2)}, u32[]{:S(2)}) collective-permute-start(bf16[2,64,1536]{2,1,0:T(8,128)(2,1)S(1)} %pad_maximum_fusion), channel_id=1, source_target_pairs={{2,0},{4,2},{6,4},{8,6},{10,8},{12,10},{14,12},{3,1},{5,3},{7,5},{... | collective-permute-start | bytes 1179656 | tf_op jit(solution)/shard_map/ppermute | solution.py:13
  171.3 9.1 %collective-permute-start = (bf16[2,64,1536]{2,1,0:T(8,128)(2,1)S(1)}, bf16[2,64,1536]{2,1,0:T(8,128)(2,1)S(1)}, u32[]{:S(2)}, u32[]{:S(2)}) collective-permute-start(bf16[2,64,1536]{2,1,0:T(8,128)(2,1)S(1)} %pad_maximum_fusion), channel_id=1, source_target_pairs={{0,2},{2,4},{4,6},{6,8},{8,10},{10,12},{12,14},{1,3},{3,5},{5,7},{... | collective-permute-start | bytes 1179656 | tf_op jit(solution)/shard_map/ppermute | solution.py:13
  180.4 0.9 copy-start.13
  181.3 0.9 copy-start.11
  186.5 7.6 %collective-permute-start.2 = (bf16[64,1536]{1,0:T(8,128)(2,1)S(1)}, bf16[64,1536]{1,0:T(8,128)(2,1)S(1)}, u32[]{:S(2)}, u32[]{:S(2)}) collective-permute-start(bf16[64,1536]{1,0:T(8,128)(2,1)S(1)} %get-tuple-element.108), channel_id=1, source_target_pairs={{0,1},{2,3},{4,5},{6,7},{8,9},{10,11},{12,13},{14,15},{16,17},{18,... | collective-permute-start | bytes 589832 | tf_op jit(solution)/shard_map/ppermute | solution.py:13
  201.9 1.1 copy-start.4
  203.0 1.1 slice-start.2
  204.6 5.5 %copy-start.5 = (f32[64,3,12,128]{3,0,2,1:T(8,128)S(1)}, f32[64,3,12,128]{3,0,2,1:T(8,128)}, u32[]{:S(2)}) copy-start(f32[64,3,12,128]{3,0,2,1:T(8,128)} %copy-done.4) | copy-start | bytes 3538948
  205.7 7.2 %collective-permute-start.4 = (bf16[2,64,1536]{2,1,0:T(8,128)(2,1)S(1)}, bf16[2,64,1536]{2,1,0:T(8,128)(2,1)S(1)}, u32[]{:S(2)}, u32[]{:S(2)}) collective-permute-start(bf16[2,64,1536]{2,1,0:T(8,128)(2,1)S(1)} %pad_maximum_fusion.1), channel_id=1, source_target_pairs={{2,0},{4,2},{6,4},{8,6},{10,8},{12,10},{14,12},{3,1},{5,3},{7,5},{... | collective-permute-start | bytes 1179656 | tf_op jit(solution)/shard_map/ppermute | solution.py:13
  207.7 9.2 %collective-permute-start.3 = (bf16[2,64,1536]{2,1,0:T(8,128)(2,1)S(1)}, bf16[2,64,1536]{2,1,0:T(8,128)(2,1)}, u32[]{:S(2)}, u32[]{:S(2)}) collective-permute-start(bf16[2,64,1536]{2,1,0:T(8,128)(2,1)S(1)} %pad_maximum_fusion.1), channel_id=1, source_target_pairs={{0,2},{2,4},{4,6},{6,8},{8,10},{10,12},{12,14},{1,3},{3,5},{5,7},{... | collective-permute-start | bytes 1179656 | tf_op jit(solution)/shard_map/ppermute | solution.py:13
  218.4 1.6 copy-start.9
  218.4 1.6 copy-start.12
  224.3 7.6 %collective-permute-start.5 = (bf16[64,1536]{1,0:T(8,128)(2,1)S(1)}, bf16[64,1536]{1,0:T(8,128)(2,1)S(1)}, u32[]{:S(2)}, u32[]{:S(2)}) collective-permute-start(bf16[64,1536]{1,0:T(8,128)(2,1)S(1)} %get-tuple-element.110), channel_id=1, source_target_pairs={{0,1},{2,3},{4,5},{6,7},{8,9},{10,11},{12,13},{14,15},{16,17},{18,... | collective-permute-start | bytes 589832 | tf_op jit(solution)/shard_map/ppermute | solution.py:13
  239.7 1.1 copy-start
  240.8 1.0 slice-start
  242.3 4.7 %copy-start.1 = (f32[64,3,12,128]{3,0,2,1:T(8,128)S(1)}, f32[64,3,12,128]{3,0,2,1:T(8,128)}, u32[]{:S(2)}) copy-start(f32[64,3,12,128]{3,0,2,1:T(8,128)} %copy-done) | copy-start | bytes 3538948
  242.5 7.3 %collective-permute-start.7 = (bf16[2,64,1536]{2,1,0:T(8,128)(2,1)S(1)}, bf16[2,64,1536]{2,1,0:T(8,128)(2,1)S(1)}, u32[]{:S(2)}, u32[]{:S(2)}) collective-permute-start(bf16[2,64,1536]{2,1,0:T(8,128)(2,1)S(1)} %pad_maximum_fusion.2), channel_id=1, source_target_pairs={{2,0},{4,2},{6,4},{8,6},{10,8},{12,10},{14,12},{3,1},{5,3},{7,5},{... | collective-permute-start | bytes 1179656 | tf_op jit(solution)/shard_map/ppermute | solution.py:13
  244.5 9.1 %collective-permute-start.6 = (bf16[2,64,1536]{2,1,0:T(8,128)(2,1)S(1)}, bf16[2,64,1536]{2,1,0:T(8,128)(2,1)S(1)}, u32[]{:S(2)}, u32[]{:S(2)}) collective-permute-start(bf16[2,64,1536]{2,1,0:T(8,128)(2,1)S(1)} %pad_maximum_fusion.2), channel_id=1, source_target_pairs={{0,2},{2,4},{4,6},{6,8},{8,10},{10,12},{12,14},{1,3},{3,5},{5,7},{... | collective-permute-start | bytes 1179656 | tf_op jit(solution)/shard_map/ppermute | solution.py:13
  253.6 0.9 copy-start.7
  254.6 1.6 copy-start.8
  254.6 1.6 copy-start.10
Sparse Core Ops, SparseCore 0:
  9.0 128.0 all-gather.2
where the time goes:
time: 269 us; the launch traced here: 268 us
  waiting for transfers between devices  134 us (50%)
  matrix products  40 us (15%)
  local copies, waits for them, and re-layouts  35.9 us (13%)
  between operations  31.1 us (12%)
  starting transfers between devices  18.7 us (7%)
  other arithmetic  8.29 us (3%)
    all_gather x1, waiting for transfers between devices, body(): whole_qkv = lax.all_gather(qkv_weight[0], 'seq', axis=0, tiled=True)  111 us
    dot_general x3, matrix products, body(): jnp.dot(lax.all_gather(normed, 'tp', axis=1, tiled=True), qkv_flat, prefe...  22.7 us
    ppermute x8, waiting for transfers between devices, shifted(): return lax.ppermute(array, axis, pairs)  22.2 us
    all_gather x1, local copies, waits for them, and re-layouts, body(): whole_qkv = lax.all_gather(qkv_weight[0], 'seq', axis=0, tiled=True)  18.7 us
    ppermute x8, starting transfers between devices, shifted(): return lax.ppermute(array, axis, pairs)  18.7 us
    dot_general x3, matrix products, body(): jnp.dot(lax.all_gather(attended, 'tp', axis=1, tiled=True), out_rows, pre...  12.5 us
  transfers between devices with their start and end apart: 9, of which 9 were waited for; matrix products, arithmetic and copies ran while one was open for 5% of the time, Pallas kernels for 0%

commit v1 on v0

--- a/solution.py
+++ b/solution.py
@@ -43,7 +43,21 @@
     seq_place = lax.axis_index("seq")
     section_place = lax.axis_index("section")
     full_width = local_width * lax.axis_size("tp")
-    whole_qkv = lax.all_gather(qkv_weight[0], "seq", axis=0, tiled=True)
+    ways, here, step = (lax.axis_size("seq"), lax.axis_index("seq"), qkv_weight[0].shape[0])
+    shape = [n * ways if d == 0 else n for d, n in enumerate(qkv_weight[0].shape)]
+    full = lax.dynamic_update_slice_in_dim(
+        jnp.zeros(shape, qkv_weight[0].dtype), qkv_weight[0], here * step, axis=0
+    )
+    going_up = going_down = qkv_weight[0]
+    for far in range(1, ways // 2 + 1):
+        going_up = lax.ppermute(going_up, "seq", [(d, (d + 1) % ways) for d in range(ways)])
+        full = lax.dynamic_update_slice_in_dim(full, going_up, (here - far) % ways * step, axis=0)
+        if 2 * far < ways:
+            going_down = lax.ppermute(going_down, "seq", [(d, (d - 1) % ways) for d in range(ways)])
+            full = lax.dynamic_update_slice_in_dim(
+                full, going_down, (here + far) % ways * step, axis=0
+            )
+    whole_qkv = full
     qkv_flat = whole_qkv.reshape(whole_qkv.shape[0], 3 * local_width)
     gain_pair = norm_gain[0]
     out_rows = out_weight[0]

time: 269 us -> 458 us (1.70)
  the two profiles are of different devices: /device:TPU:10 before, /device:TPU:15 now
where the time goes in v1:
time: 458 us; the launch traced here: 452 us
  local copies, waits for them, and re-layouts  226 us (49%)
  waiting for transfers between devices  129 us (28%)
  matrix products  39 us (9%)
  starting transfers between devices  30.1 us (7%)
  between operations  18.2 us (4%)
  other arithmetic  9.63 us (2%)
    ppermute x4, waiting for transfers between devices, body(): lax.ppermute(going_up, 'seq', [(d, (d + 1) % ways) for d in range(ways)])  107 us
    dynamic_update_slice x4, local copies, waits for them, and re-layouts, body(): lax.dynamic_update_slice_in_dim(full, going_up, (here - far) % ways * ste...  91.3 us
    dynamic_update_slice x3, local copies, waits for them, and re-layouts, body(): lax.dynamic_update_slice_in_dim(full, going_down, (here + far) % ways * s...  67.3 us
    dynamic_update_slice x1, local copies, waits for them, and re-layouts, body(): lax.dynamic_update_slice_in_dim(jnp.zeros(shape, qkv_weight[0].dtype), qk...  24.4 us
    dot_general x3, matrix products, body(): jnp.dot(lax.all_gather(normed, 'tp', axis=1, tiled=True), qkv_flat, prefe...  22.7 us
    ppermute x8, waiting for transfers between devices, shifted(): return lax.ppermute(array, axis, pairs)  22.5 us
    ppermute x8, starting transfers between devices, shifted(): return lax.ppermute(array, axis, pairs)  18 us
    dot_general x3, matrix products, body(): jnp.dot(lax.all_gather(attended, 'tp', axis=1, tiled=True), out_rows, pre...  12.5 us
  transfers between devices with their start and end apart: 15, of which 11 were waited for; matrix products, arithmetic and copies ran while one was open for 44% of the time, Pallas kernels for 0%

profile of v1, /device:TPU:15, one launch (start us, length us, event | category | flops | bytes accessed | tf_op | source)
XLA Modules:
  0.0 452.2 jit_solution(1176704365144102347)
XLA Ops:
  1.9 36.1 %collective-permute-done = bf16[192,3,1536]{2,0,1:T(8,128)(2,1)S(1)} collective-permute-done((bf16[192,3,1536]{2,0,1:T(8,128)(2,1)}, bf16[192,3,1536]{2,0,1:T(8,128)(2,1)S(1)}, u32[]{:S(2)}, u32[]{:S(2)}) %collective-permute-start) | collective-permute-done | bytes 1769504 | tf_op jit(solution)/shard_map/ppermute | solution.py:53
  38.0 5.0 %collective-permute-start.2 = (bf16[192,3,1536]{2,0,1:T(8,128)(2,1)S(1)}, bf16[192,3,1536]{2,0,1:T(8,128)(2,1)S(1)}, u32[]{:S(2)}, u32[]{:S(2)}) collective-permute-start(bf16[192,3,1536]{2,0,1:T(8,128)(2,1)S(1)} %collective-permute-done), channel_id=1, source_target_pairs={{0,2},{2,4},{4,6},{6,8},{8,10},{10,12},{12,14},{14,0},{1,3},{3,5},... | collective-permute-start | bytes 5308424 | tf_op jit(solution)/shard_map/ppermute | solution.py:53
  43.0 38.4 %collective-permute-done.2 = bf16[192,3,1536]{2,0,1:T(8,128)(2,1)S(1)} collective-permute-done((bf16[192,3,1536]{2,0,1:T(8,128)(2,1)S(1)}, bf16[192,3,1536]{2,0,1:T(8,128)(2,1)S(1)}, u32[]{:S(2)}, u32[]{:S(2)}) %collective-permute-start.2) | collective-permute-done | bytes 1769504 | tf_op jit(solution)/shard_map/ppermute | solution.py:53
  87.9 32.0 %collective-permute-done.4 = bf16[192,3,1536]{2,0,1:T(8,128)(2,1)} collective-permute-done((bf16[192,3,1536]{2,0,1:T(8,128)(2,1)S(1)}, bf16[192,3,1536]{2,0,1:T(8,128)(2,1)}, u32[]{:S(2)}, u32[]{:S(2)}) %collective-permute-start.4) | collective-permute-done | bytes 1769504 | tf_op jit(solution)/shard_map/ppermute | solution.py:53
  119.9 2.7 collective-permute-start.6
  122.8 2.7 copy.67
  141.2 6.2 %broadcast_in_dim.20 = bf16[1536,3,1536]{0,2,1:T(8,128)(2,1)} broadcast(bf16[]{:T(256)} %constant.151.clone.1), dimensions={} | broadcast | bytes 14155778 | tf_op jit(solution)/shard_map/broadcast_in_dim | solution.py:49
  147.4 24.4 %dynamic_update_slice.24 = bf16[1536,3,1536]{0,2,1:T(8,128)(2,1)} dynamic-update-slice(bf16[1536,3,1536]{0,2,1:T(8,128)(2,1)} %broadcast_in_dim.20, bf16[192,3,1536]{0,2,1:T(8,128)(2,1)S(1)} %bitcast.259, s32[]{:T(128)S(6)} %select_n.146, s32[]{:T(128)} %constant.152.clone.1, s32[]{:T(128)} %constant.152.clone.1) | dynamic-update-slice | bytes 3538948 | tf_op jit(solution)/shard_map/dynamic_update_slice | solution.py:48
  173.9 2.7 copy.69
  176.6 21.8 %dynamic_update_slice.25 = bf16[1536,3,1536]{0,2,1:T(8,128)(2,1)} dynamic-update-slice(bf16[1536,3,1536]{0,2,1:T(8,128)(2,1)} %dynamic_update_slice.24, bf16[192,3,1536]{0,2,1:T(8,128)(2,1)S(1)} %copy.69, s32[]{:T(128)S(6)} %select_n.148, s32[]{:T(128)} %constant.152.clone.1, s32[]{:T(128)} %constant.152.clone.1) | dynamic-update-slice | bytes 3538948 | tf_op jit(solution)/shard_map/dynamic_update_slice | solution.py:54
  198.4 2.7 copy.71
  201.0 21.9 %dynamic_update_slice.26 = bf16[1536,3,1536]{0,2,1:T(8,128)(2,1)} dynamic-update-slice(bf16[1536,3,1536]{0,2,1:T(8,128)(2,1)} %dynamic_update_slice.25, bf16[192,3,1536]{0,2,1:T(8,128)(2,1)S(1)} %copy.71, s32[]{:T(128)S(6)} %select_n.150, s32[]{:T(128)} %constant.152.clone.1, s32[]{:T(128)} %constant.152.clone.1) | dynamic-update-slice | bytes 3538948 | tf_op jit(solution)/shard_map/dynamic_update_slice | solution.py:57
  222.9 2.7 copy.72
  225.6 24.4 %dynamic_update_slice.27 = bf16[1536,3,1536]{0,2,1:T(8,128)(2,1)} dynamic-update-slice(bf16[1536,3,1536]{0,2,1:T(8,128)(2,1)} %dynamic_update_slice.26, bf16[192,3,1536]{0,2,1:T(8,128)(2,1)S(1)} %copy.72, s32[]{:T(128)S(6)} %select_n.152, s32[]{:T(128)} %constant.152.clone.1, s32[]{:T(128)} %constant.152.clone.1) | dynamic-update-slice | bytes 3538948 | tf_op jit(solution)/shard_map/dynamic_update_slice | solution.py:54
  252.7 24.4 %dynamic_update_slice.28 = bf16[1536,3,1536]{0,2,1:T(8,128)(2,1)} dynamic-update-slice(bf16[1536,3,1536]{0,2,1:T(8,128)(2,1)} %dynamic_update_slice.27, bf16[192,3,1536]{0,2,1:T(8,128)(2,1)S(1)} %copy.73, s32[]{:T(128)S(6)} %select_n.154, s32[]{:T(128)} %constant.152.clone.1, s32[]{:T(128)} %constant.152.clone.1) | dynamic-update-slice | bytes 3538948 | tf_op jit(solution)/shard_map/dynamic_update_slice | solution.py:57
  279.7 21.7 %dynamic_update_slice.29 = bf16[1536,3,1536]{0,2,1:T(8,128)(2,1)} dynamic-update-slice(bf16[1536,3,1536]{0,2,1:T(8,128)(2,1)} %dynamic_update_slice.28, bf16[192,3,1536]{0,2,1:T(8,128)(2,1)S(1)} %copy.74, s32[]{:T(128)S(6)} %select_n.156, s32[]{:T(128)} %constant.152.clone.1, s32[]{:T(128)} %constant.152.clone.1) | dynamic-update-slice | bytes 3538948 | tf_op jit(solution)/shard_map/dynamic_update_slice | solution.py:54
  301.4 2.7 copy.75
  304.1 21.1 %dynamic_update_slice.30 = bf16[1536,3,1536]{0,2,1:T(8,128)(2,1)} dynamic-update-slice(bf16[1536,3,1536]{0,2,1:T(8,128)(2,1)} %dynamic_update_slice.29, bf16[192,3,1536]{0,2,1:T(8,128)(2,1)S(1)} %copy.75, s32[]{:T(128)S(6)} %select_n.158, s32[]{:T(128)} %constant.152.clone.1, s32[]{:T(128)} %constant.152.clone.1) | dynamic-update-slice | bytes 3538948 | tf_op jit(solution)/shard_map/dynamic_update_slice | solution.py:57
  325.2 2.7 copy.76
  327.9 23.5 %dynamic_update_slice.31 = bf16[1536,3,1536]{0,2,1:T(8,128)(2,1)} dynamic-update-slice(bf16[1536,3,1536]{0,2,1:T(8,128)(2,1)} %dynamic_update_slice.30, bf16[192,3,1536]{0,2,1:T(8,128)(2,1)S(1)} %copy.76, s32[]{:T(128)S(6)} %select_n.160, s32[]{:T(128)} %constant.152.clone.1, s32[]{:T(128)} %constant.152.clone.1) | dynamic-update-slice | bytes 3538948 | tf_op jit(solution)/shard_map/dynamic_update_slice | solution.py:54
  351.4 7.5 %fusion.129 = f32[64,3,12,128]{3,0,2,1:T(8,128)S(1)} fusion(bf16[3,12,128,1536]{3,2,1,0:T(8,128)(2,1)} %bitcast.256, f32[1536]{0:T(1024)S(1)} %get-tuple-element.59, f32[1536]{0:T(1024)S(1)} %get-tuple-element.58, f32[64]{0:T(128)S(1)} %get-tuple-element.102, f32[64]{0:T(128)S(1)} %get-tuple-element.101, bf16[2,64,1536]{2,1,0:T(8,128)(2,1)S(1)} %copy-done, ...), kind=kOutput, calls=%fused_computation.139 | convolution fusion | flops 906657792 | bytes 15549441 | tf_op jit(solution)/shard_map/dot_general | solution.py:86
  367.2 4.2 collective-permute-done.8
  373.5 3.9 bitcast_dynamic-update-slice_fusion
  385.2 7.6 %fusion.126 = f32[64,3,12,128]{3,0,2,1:T(8,128)S(1)} fusion(bf16[3,12,128,1536]{3,2,1,0:T(8,128)(2,1)} %bitcast.257, bf16[64,1536]{1,0:T(8,128)(2,1)S(1)} %get-tuple-element.63, f32[1536]{0:T(1024)S(1)} %get-tuple-element.57, f32[1536]{0:T(1024)S(1)} %get-tuple-element.56, f32[64]{0:T(128)S(1)} %get-tuple-element.96, f32[64]{0:T(128)S(1)} %get-tuple-element.95), kind=kOutput, calls=%fused_computation.137 | convolution fusion | flops 906559488 | bytes 15544832 | tf_op jit(solution)/shard_map/dot_general | solution.py:86
  395.8 3.0 collective-permute-start.10
  403.7 4.3 collective-permute-done.11
  411.6 4.0 fusion.121
  417.9 5.0 %collective-permute-done.12 = bf16[64,1536]{1,0:T(8,128)(2,1)S(1)} collective-permute-done((bf16[64,1536]{1,0:T(8,128)(2,1)S(1)}, bf16[64,1536]{1,0:T(8,128)(2,1)S(1)}, u32[]{:S(2)}, u32[]{:S(2)}) %collective-permute-start.12) | collective-permute-done | bytes 196640 | tf_op jit(solution)/shard_map/ppermute | solution.py:13
  423.1 7.6 %fusion.123 = f32[64,3,12,128]{3,0,2,1:T(8,128)S(1)} fusion(bf16[3,12,128,1536]{3,2,1,0:T(8,128)(2,1)} %bitcast.258, bf16[64,1536]{1,0:T(8,128)(2,1)S(1)} %get-tuple-element.62, f32[1536]{0:T(1024)S(1)} %get-tuple-element.55, f32[1536]{0:T(1024)S(1)} %get-tuple-element.54, f32[64]{0:T(128)S(1)} %get-tuple-element.89, f32[64]{0:T(128)S(1)} %get-tuple-element.88), kind=kOutput, calls=%fused_computation.135 | convolution fusion | flops 906559488 | bytes 15544832 | tf_op jit(solution)/shard_map/dot_general | solution.py:86
  432.1 3.9 collective-permute-start.13
  441.7 3.5 collective-permute-done.14
  447.6 4.6 %fusion.45 = bf16[1,2,64,1536]{3,2,1,0:T(8,128)(2,1)} fusion(bf16[1,2,64,1536]{3,2,1,0:T(8,128)(2,1)} %copy.138, s32[]{:T(128)} %min.38, bf16[1,1536,1536]{2,1,0:T(8,128)(2,1)} %param.19, bf16[64,1536]{1,0:T(8,128)(2,1)S(1)} %get-tuple-element.62, bf16[12,8,8,128]{3,2,1,0:T(8,128)(2,1)S(1)} %fusion.62, bf16[2,64,1536]{2,1,0:T(8,128)(2,1)S(1)} %get-tuple-element.109, ...), kind=kOutput, calls=%fused_computation.19 | convolution fusion | flops 302579712 | bytes 5512193 | tf_op jit(solution)/shard_map/dot_general | solution.py:132
  (170 shorter events, 55.5 us)
Async XLA Ops:
  0.0 38.0 %collective-permute-start = (bf16[192,3,1536]{2,0,1:T(8,128)(2,1)}, bf16[192,3,1536]{2,0,1:T(8,128)(2,1)S(1)}, u32[]{:S(2)}, u32[]{:S(2)}) collective-permute-start(bf16[192,3,1536]{2,0,1:T(8,128)(2,1)} %bitcast.261), channel_id=1, source_target_pairs={{0,2},{2,4},{4,6},{6,8},{8,10},{10,12},{12,14},{14,0},{1,3},{3,5},... | collective-permute-start | bytes 5308424 | tf_op jit(solution)/shard_map/ppermute | solution.py:53
  1.9 41.1 %collective-permute-start.1 = (bf16[192,3,1536]{2,0,1:T(8,128)(2,1)}, bf16[192,3,1536]{2,0,1:T(8,128)(2,1)S(1)}, u32[]{:S(2)}, u32[]{:S(2)}) collective-permute-start(bf16[192,3,1536]{2,0,1:T(8,128)(2,1)} %bitcast.262), channel_id=1, source_target_pairs={{0,14},{2,0},{4,2},{6,4},{8,6},{10,8},{12,10},{14,12},{1,15},{3,1}... | collective-permute-start | bytes 5308424 | tf_op jit(solution)/shard_map/ppermute | solution.py:56
  38.0 43.5 %copy-start.3 = (bf16[192,3,1536]{2,0,1:T(8,128)(2,1)}, bf16[192,3,1536]{2,0,1:T(8,128)(2,1)S(1)}, u32[]{:S(2)}) copy-start(bf16[192,3,1536]{2,0,1:T(8,128)(2,1)S(1)} %collective-permute-done) | copy-start | bytes 5308420
  38.0 43.4 %collective-permute-start.2 = (bf16[192,3,1536]{2,0,1:T(8,128)(2,1)S(1)}, bf16[192,3,1536]{2,0,1:T(8,128)(2,1)S(1)}, u32[]{:S(2)}, u32[]{:S(2)}) collective-permute-start(bf16[192,3,1536]{2,0,1:T(8,128)(2,1)S(1)} %collective-permute-done), channel_id=1, source_target_pairs={{0,2},{2,4},{4,6},{6,8},{8,10},{10,12},{12,14},{14,0},{1,3},{3,5},... | collective-permute-start | bytes 5308424 | tf_op jit(solution)/shard_map/ppermute | solution.py:53
  43.0 79.8 %copy-start.1 = (bf16[192,3,1536]{2,0,1:T(8,128)(2,1)}, bf16[192,3,1536]{2,0,1:T(8,128)(2,1)S(1)}, u32[]{:S(2)}) copy-start(bf16[192,3,1536]{2,0,1:T(8,128)(2,1)S(1)} %collective-permute-done.1) | copy-start | bytes 5308420
  43.0 44.9 %collective-permute-start.3 = (bf16[192,3,1536]{2,0,1:T(8,128)(2,1)S(1)}, bf16[192,3,1536]{2,0,1:T(8,128)(2,1)}, u32[]{:S(2)}, u32[]{:S(2)}) collective-permute-start(bf16[192,3,1536]{2,0,1:T(8,128)(2,1)S(1)} %collective-permute-done.1), channel_id=1, source_target_pairs={{0,14},{2,0},{4,2},{6,4},{8,6},{10,8},{12,10},{14,12},{1,15},{3,1}... | collective-permute-start | bytes 5308424 | tf_op jit(solution)/shard_map/ppermute | solution.py:56
  81.4 41.3 %copy-start.2 = (bf16[192,3,1536]{2,0,1:T(8,128)(2,1)}, bf16[192,3,1536]{2,0,1:T(8,128)(2,1)S(1)}, u32[]{:S(2)}) copy-start(bf16[192,3,1536]{2,0,1:T(8,128)(2,1)S(1)} %collective-permute-done.2) | copy-start | bytes 5308420
  81.4 38.5 %collective-permute-start.4 = (bf16[192,3,1536]{2,0,1:T(8,128)(2,1)S(1)}, bf16[192,3,1536]{2,0,1:T(8,128)(2,1)}, u32[]{:S(2)}, u32[]{:S(2)}) collective-permute-start(bf16[192,3,1536]{2,0,1:T(8,128)(2,1)S(1)} %collective-permute-done.2), channel_id=1, source_target_pairs={{0,2},{2,4},{4,6},{6,8},{8,10},{10,12},{12,14},{14,0},{1,3},{3,5},... | collective-permute-start | bytes 5308424 | tf_op jit(solution)/shard_map/ppermute | solution.py:53
  87.9 213.5 %collective-permute-start.5 = (bf16[192,3,1536]{2,0,1:T(8,128)(2,1)}, bf16[192,3,1536]{2,0,1:T(8,128)(2,1)}, u32[]{:S(2)}, u32[]{:S(2)}) collective-permute-start(bf16[192,3,1536]{2,0,1:T(8,128)(2,1)} %collective-permute-done.3), channel_id=1, source_target_pairs={{0,14},{2,0},{4,2},{6,4},{8,6},{10,8},{12,10},{14,12},{1,15},{3,1}... | collective-permute-start | bytes 5308424 | tf_op jit(solution)/shard_map/ppermute | solution.py:56
  119.9 205.3 %collective-permute-start.6 = (bf16[192,3,1536]{2,0,1:T(8,128)(2,1)}, bf16[192,3,1536]{2,0,1:T(8,128)(2,1)}, u32[]{:S(2)}, u32[]{:S(2)}) collective-permute-start(bf16[192,3,1536]{2,0,1:T(8,128)(2,1)} %collective-permute-done.4), channel_id=1, source_target_pairs={{0,2},{2,4},{4,6},{6,8},{8,10},{10,12},{12,14},{14,0},{1,3},{3,5},... | collective-permute-start | bytes 5308424 | tf_op jit(solution)/shard_map/ppermute | solution.py:53
  147.4 24.4 %copy-start.9 = (bf16[1,2,6,1536]{3,1,2,0:T(2,128)(2,1)S(1)}, bf16[1,2,6,1536]{3,1,2,0:T(2,128)(2,1)}, u32[]{:S(2)}) copy-start(bf16[1,2,6,1536]{3,1,2,0:T(2,128)(2,1)} %param.16) | copy-start | bytes 110596
  147.4 24.5 %copy-start.11 = (s32[3]{0:T(128)S(1)}, s32[3]{0:T(128)}, u32[]{:S(2)}) copy-start(s32[3]{0:T(128)} %constant.157.clone.1) | copy-start | bytes 40
  147.4 26.1 %copy-start = (bf16[2,64,1536]{2,1,0:T(8,128)(2,1)S(1)}, bf16[2,64,1536]{2,1,0:T(8,128)(2,1)}, u32[]{:S(2)}) copy-start(bf16[2,64,1536]{2,1,0:T(8,128)(2,1)} %param.13) | copy-start | bytes 1179652
  147.4 26.4 %copy-start.10 = (f32[1,2,128]{2,1,0:T(2,128)S(1)}, f32[1,2,128]{2,1,0:T(2,128)}, u32[]{:S(2)}) copy-start(f32[1,2,128]{2,1,0:T(2,128)} %param.18) | copy-start | bytes 3076
  360.3 6.6 %collective-permute-start.7 = (bf16[2,64,1536]{2,1,0:T(8,128)(2,1)S(1)}, bf16[2,64,1536]{2,1,0:T(8,128)(2,1)S(1)}, u32[]{:S(2)}, u32[]{:S(2)}) collective-permute-start(bf16[2,64,1536]{2,1,0:T(8,128)(2,1)S(1)} %pad_maximum_fusion), channel_id=1, source_target_pairs={{0,2},{2,4},{4,6},{6,8},{8,10},{10,12},{12,14},{1,3},{3,5},{5,7},{... | collective-permute-start | bytes 1179656 | tf_op jit(solution)/shard_map/ppermute | solution.py:13
  362.3 9.2 %collective-permute-start.8 = (bf16[2,64,1536]{2,1,0:T(8,128)(2,1)S(1)}, bf16[2,64,1536]{2,1,0:T(8,128)(2,1)S(1)}, u32[]{:S(2)}, u32[]{:S(2)}) collective-permute-start(bf16[2,64,1536]{2,1,0:T(8,128)(2,1)S(1)} %pad_maximum_fusion), channel_id=1, source_target_pairs={{2,0},{4,2},{6,4},{8,6},{10,8},{12,10},{14,12},{3,1},{5,3},{7,5},{... | collective-permute-start | bytes 1179656 | tf_op jit(solution)/shard_map/ppermute | solution.py:13
  371.6 0.9 copy-start.8
  377.4 7.5 %collective-permute-start.9 = (bf16[64,1536]{1,0:T(8,128)(2,1)S(1)}, bf16[64,1536]{1,0:T(8,128)(2,1)S(1)}, u32[]{:S(2)}, u32[]{:S(2)}) collective-permute-start(bf16[64,1536]{1,0:T(8,128)(2,1)S(1)} %get-tuple-element.108), channel_id=1, source_target_pairs={{0,1},{2,3},{4,5},{6,7},{8,9},{10,11},{12,13},{14,15},{16,17},{18,... | collective-permute-start | bytes 589832 | tf_op jit(solution)/shard_map/ppermute | solution.py:13
  395.8 7.7 %collective-permute-start.10 = (bf16[2,64,1536]{2,1,0:T(8,128)(2,1)S(1)}, bf16[2,64,1536]{2,1,0:T(8,128)(2,1)S(1)}, u32[]{:S(2)}, u32[]{:S(2)}) collective-permute-start(bf16[2,64,1536]{2,1,0:T(8,128)(2,1)S(1)} %pad_maximum_fusion.1), channel_id=1, source_target_pairs={{0,2},{2,4},{4,6},{6,8},{8,10},{10,12},{12,14},{1,3},{3,5},{5,7},{... | collective-permute-start | bytes 1179656 | tf_op jit(solution)/shard_map/ppermute | solution.py:13
  398.7 9.2 %collective-permute-start.11 = (bf16[2,64,1536]{2,1,0:T(8,128)(2,1)S(1)}, bf16[2,64,1536]{2,1,0:T(8,128)(2,1)}, u32[]{:S(2)}, u32[]{:S(2)}) collective-permute-start(bf16[2,64,1536]{2,1,0:T(8,128)(2,1)S(1)} %pad_maximum_fusion.1), channel_id=1, source_target_pairs={{2,0},{4,2},{6,4},{8,6},{10,8},{12,10},{14,12},{3,1},{5,3},{7,5},{... | collective-permute-start | bytes 1179656 | tf_op jit(solution)/shard_map/ppermute | solution.py:13
  409.6 1.6 copy-start.6
  415.6 7.4 %collective-permute-start.12 = (bf16[64,1536]{1,0:T(8,128)(2,1)S(1)}, bf16[64,1536]{1,0:T(8,128)(2,1)S(1)}, u32[]{:S(2)}, u32[]{:S(2)}) collective-permute-start(bf16[64,1536]{1,0:T(8,128)(2,1)S(1)} %get-tuple-element.110), channel_id=1, source_target_pairs={{0,1},{2,3},{4,5},{6,7},{8,9},{10,11},{12,13},{14,15},{16,17},{18,... | collective-permute-start | bytes 589832 | tf_op jit(solution)/shard_map/ppermute | solution.py:13
  432.1 8.6 %collective-permute-start.13 = (bf16[2,64,1536]{2,1,0:T(8,128)(2,1)S(1)}, bf16[2,64,1536]{2,1,0:T(8,128)(2,1)S(1)}, u32[]{:S(2)}, u32[]{:S(2)}) collective-permute-start(bf16[2,64,1536]{2,1,0:T(8,128)(2,1)S(1)} %pad_maximum_fusion.2), channel_id=1, source_target_pairs={{0,2},{2,4},{4,6},{6,8},{8,10},{10,12},{12,14},{1,3},{3,5},{5,7},{... | collective-permute-start | bytes 1179656 | tf_op jit(solution)/shard_map/ppermute | solution.py:13
  436.0 9.1 %collective-permute-start.14 = (bf16[2,64,1536]{2,1,0:T(8,128)(2,1)S(1)}, bf16[2,64,1536]{2,1,0:T(8,128)(2,1)S(1)}, u32[]{:S(2)}, u32[]{:S(2)}) collective-permute-start(bf16[2,64,1536]{2,1,0:T(8,128)(2,1)S(1)} %pad_maximum_fusion.2), channel_id=1, source_target_pairs={{2,0},{4,2},{6,4},{8,6},{10,8},{12,10},{14,12},{3,1},{5,3},{7,5},{... | collective-permute-start | bytes 1179656 | tf_op jit(solution)/shard_map/ppermute | solution.py:13
  445.3 0.9 copy-start.4
  445.3 1.0 copy-start.7
  446.4 0.9 copy-start.5
